TPU v7x, 256 devices: a whole 4x4x8 slice. The times are simulated.
256 devices in a mesh: dp: 32 (over x, z), seq: 8 (over y, core).
Axes of the slice: x: 4, y: 4, z: 8, core: 2. Of those that a mesh axis runs over, the one named last changes fastest.
Arguments:
- span_store: bfloat16 [32, 512, 8192], P('dp', 'seq'), may hold values from -6 to 6
- target: int32 [32, 512], P('dp', 'seq'), may hold values from 0 to 31, as said below
- segment_ids: int32 [32, 512], P('dp'), may hold values from 0 to 7, never falling along the last dimension, each value on 1 to 128 neighbouring positions
- norm_gain: float32 [8192], replicated, may hold values from 0.25 to 1.75
- w_query: bfloat16 [8192, 4096], P('dp', 'seq'), may hold values from -0.0625 to 0.0625
- key_weight: bfloat16 [8192, 1024], P('dp', 'seq'), may hold values from -0.0625 to 0.0625
- value_weight: bfloat16 [8192, 1024], P('dp', 'seq'), may hold values from -0.0625 to 0.0625
Outputs:
- context: bfloat16 [32, 512, 4096], P('dp', 'seq')
Inputs may be any that keep to these rules, and one draw needn't show every extreme that they name: `target`: within one lane, the stored tokens of all shards that name one packed row number exactly 64; one shard's tokens of one lane name one row at most 3 times, and exactly 3 times for some shard and row in every lane. `segment_ids`: along a row, document ids never fall.
All inputs are finite; a program needn't handle non-finite values.
Results may differ from a plain program's by a relative error of at most 0.0079.
Values may be sent and summed in bfloat16 or wider, within the bound.
No kernel may reach another device: no remote copies, remote signals or barrier semaphores. Data moves between devices by JAX's collectives and lax.ppermute only.
A program may use at most 128 MiB of HBM per device.

v0:
```python
import jax
import jax.numpy as jnp
from jax import lax
from jax.sharding import PartitionSpec as P

HEAD_SIZE = 128
epsilon = 1e-05
rope_base = 500000.0


def rotary_angles(values, token_positions):
    half_dim = values.shape[-1] // 2
    exponent = jnp.arange(half_dim, dtype=jnp.float32) * (2.0 / values.shape[-1])
    frequency = rope_base ** (-exponent)
    angles = token_positions.astype(jnp.float32)[:, None] * frequency[None, :]
    cosine = jnp.concatenate([jnp.cos(angles), jnp.cos(angles)], axis=-1)[:, None, :]
    sine_part = jnp.concatenate([jnp.sin(angles), jnp.sin(angles)], axis=-1)[:, None, :]
    rotated = jnp.concatenate([-values[..., half_dim:], values[..., :half_dim]], axis=-1)
    return values * cosine + rotated * sine_part


def normalize(block, norm_gain):
    values = block.astype(jnp.float32)
    inverse = lax.rsqrt(jnp.mean(values * values, axis=-1, keepdims=True) + epsilon)
    return (values * inverse * norm_gain).astype(jnp.bfloat16)


def shards(span_store, target, segment_ids, norm_gain, w_query, key_weight, value_weight):
    dp_count = lax.axis_size("dp")
    stored = span_store[0]
    tok_count = stored.shape[0]
    row_width = stored.shape[1]
    owners = target[0]
    onehot = (owners[:, None] == jnp.arange(dp_count, dtype=jnp.int32)[None, :]).astype(jnp.int32)
    ranking = jnp.cumsum(onehot, axis=0) - onehot
    slot_index = jnp.sum(ranking * onehot, axis=1)
    counts = jnp.sum(onehot, axis=0)
    capacity = tok_count // dp_count + tok_count // (2 * dp_count)
    outgoing = (
        jnp.zeros((dp_count, capacity, row_width), jnp.bfloat16).at[owners, slot_index].set(stored)
    )
    arrived, counts_wire = (
        lax.all_to_all(outgoing, "dp", split_axis=0, concat_axis=0, tiled=True),
        lax.all_to_all(counts.astype(jnp.bfloat16), "dp", split_axis=0, concat_axis=0, tiled=True),
    )
    got_counts = counts_wire.astype(jnp.int32)
    starts = jnp.cumsum(got_counts) - got_counts
    slot_ids = jnp.arange(capacity, dtype=jnp.int32)
    places = jnp.where(
        slot_ids[None, :] < got_counts[:, None], starts[:, None] + slot_ids[None, :], tok_count
    ).reshape(-1)
    placed = (
        jnp.zeros((tok_count, row_width), jnp.bfloat16)
        .at[places]
        .set(arrived.reshape(-1, row_width), mode="drop")
    )
    seg_all = segment_ids[0]
    length = seg_all.shape[0]
    query_cols = w_query.shape[1]
    key_cols = key_weight.shape[1]
    input_normed = lax.all_gather(normalize(placed, norm_gain), "seq", axis=0, tiled=True)
    pieces = (
        lax.all_gather(w_query, "dp", axis=0, tiled=True),
        lax.all_gather(key_weight, "dp", axis=0, tiled=True),
        lax.all_gather(value_weight, "dp", axis=0, tiled=True),
    )
    query_acc, key_acc, value_acc = tuple(
        (
            jnp.dot(input_normed, one_piece, preferred_element_type=jnp.float32)
            for one_piece in pieces
        )
    )
    groups = key_cols // HEAD_SIZE
    per_group = query_cols // key_cols
    key_pos = jnp.arange(length, dtype=jnp.int32)
    query_rows = (
        rotary_angles(query_acc.reshape(length, groups * per_group, HEAD_SIZE), key_pos)
        .astype(jnp.bfloat16)
        .reshape(length, groups, per_group, HEAD_SIZE)
    )
    key_matrix = rotary_angles(key_acc.reshape(length, groups, HEAD_SIZE), key_pos).astype(
        jnp.bfloat16
    )
    value_matrix = value_acc.astype(jnp.bfloat16).reshape(length, groups, HEAD_SIZE)
    scaling = HEAD_SIZE ** (-0.5)
    block_rows = min(512, length)
    scores = (
        jnp.einsum("qgrd,kgd->grqk", query_rows, key_matrix, preferred_element_type=jnp.float32)
        * scaling
    )
    allowed = (seg_all[:, None] == seg_all[None, :block_rows]) & (
        key_pos[None, :block_rows] <= key_pos[:, None]
    )
    exp_terms = jnp.where(allowed, jnp.exp(scores), 0.0)
    weights = (exp_terms / jnp.sum(exp_terms, axis=-1, keepdims=True)).astype(jnp.bfloat16)
    context = jnp.einsum(
        "grqk,kgd->qgrd", weights, value_matrix, preferred_element_type=jnp.float32
    )
    pieces_out = context.astype(jnp.bfloat16).reshape(block_rows, query_cols)
    returned = lax.all_to_all(pieces_out, "seq", split_axis=0, concat_axis=1, tiled=True)
    return returned[None]


def solution(mesh):
    placed = (
        P("dp", "seq", None),
        P("dp", "seq"),
        P("dp", None),
        P(),
        P("dp", "seq"),
        P("dp", "seq"),
        P("dp", "seq"),
    )
    return jax.shard_map(
        shards, mesh=mesh, in_specs=placed, out_specs=P("dp", "seq", None), check_vma=False
    )
```

profile of v0, /device:TPU:1, one launch (start us, length us, event | category | flops | bytes accessed | tf_op | source)
XLA Modules:
  0.0 389.7 jit_solution(1594310030817995858)
XLA Ops:
  6.5 0.7 all-gather.11.cloned.1.call-update
  7.3 0.7 fusion.24
  8.1 0.8 select_reduce_fusion
  8.9 0.7 copy.45
  9.7 11.9 %all-to-all-start = ((bf16[32,1,1]{2,1,0:T(2,128)(2,1)}), bf16[32,1,1]{2,1,0:T(2,128)(2,1)S(1)}, u32[]{:S(2)}, u32[]{:S(2)}) async-start(bf16[32,1,1]{2,1,0:T(2,128)(2,1)} %copy.45), calls=%async_computation | async-start | bytes 32768 | tf_op jit(solution)/shard_map/all_to_all | solution.py:44
  21.5 0.7 fusion.28
  22.3 23.9 %scatter_fusion = bf16[32,3,8192]{2,0,1:T(8,128)(2,1)S(1)} fusion(bf16[32,3,8192]{2,0,1:T(8,128)(2,1)S(1)} %broadcast_in_dim.21, s32[64]{0:T(128)S(1)} %fusion.28, bf16[64,8192]{1,0:T(8,128)(2,1)} %bitcast.80), kind=kCustom, calls=%fused_computation | custom fusion | bytes 3146240 | tf_op jit(solution)/shard_map/scatter | solution.py:40
  46.2 2.7 copy.47
  49.0 9.4 %all-to-all-start.1 = ((bf16[32,3,8192]{2,1,0:T(4,128)(2,1)}), bf16[32,3,8192]{2,1,0:T(4,128)(2,1)S(1)}, u32[]{:S(2)}, u32[]{:S(2)}) async-start(bf16[32,3,8192]{2,1,0:T(4,128)(2,1)} %copy.47), calls=%async_computation.1 | async-start | bytes 4194304 | tf_op jit(solution)/shard_map/all_to_all | solution.py:43
  59.5 62.1 %all-to-all-done.1 = bf16[32,3,8192]{2,1,0:T(4,128)(2,1)S(1)} async-done(((bf16[32,3,8192]{2,1,0:T(4,128)(2,1)}), bf16[32,3,8192]{2,1,0:T(4,128)(2,1)S(1)}, u32[]{:S(2)}, u32[]{:S(2)}) %all-to-all-start.1) | async-done | bytes 1572896 | tf_op jit(solution)/shard_map/all_to_all | solution.py:43
  121.7 2.6 reshape.239
  124.2 3.8 scatter_custom_fusion.1
  128.3 1.3 fusion.3
  129.7 0.7 all-gather.9.cloned.1.call-update
  131.8 15.4 %all-gather.11.cloned.1.call-done = bf16[8192,512]{1,0:T(8,128)(2,1)} async-done(((bf16[256,512]{1,0:T(8,128)(2,1)}), bf16[8192,512]{1,0:T(8,128)(2,1)}) %all-gather.11.cloned.1.call-update) | async-done | bytes 8388624 | tf_op jit(solution)/shard_map/all_gather | solution.py:63
  147.2 53.4 %all-gather.5.cloned.1.call-done = bf16[512,8192]{1,0:T(8,128)(2,1)} async-done(((bf16[64,8192]{1,0:T(8,128)(2,1)}), bf16[512,8192]{1,0:T(8,128)(2,1)}) %all-gather.5.cloned.1.call-update) | async-done | bytes 8388624 | tf_op jit(solution)/shard_map/all_gather | solution.py:61
  200.6 9.4 %fusion.33 = f32[512,512]{0,1:T(8,128)S(1)} fusion(bf16[512,8192]{1,0:T(8,128)(2,1)} %all-gather.5.cloned.1.call-done, bf16[8192,512]{1,0:T(8,128)(2,1)} %all-gather.11.cloned.1.call-done), kind=kOutput, calls=%fused_computation.62 | convolution fusion | flops 4294967296 | bytes 17825792 | tf_op jit(solution)/shard_map/dot_general | solution.py:69
  210.5 66.4 %all-gather.9.cloned.1.call-done = bf16[8192,128]{1,0:T(8,128)(2,1)} async-done(((bf16[256,128]{1,0:T(8,128)(2,1)}), bf16[8192,128]{1,0:T(8,128)(2,1)}) %all-gather.9.cloned.1.call-update) | async-done | bytes 2097168 | tf_op jit(solution)/shard_map/all_gather | solution.py:64
  276.9 6.8 %fusion.32 = f32[512,128]{0,1:T(8,128)S(1)} fusion(bf16[512,8192]{1,0:T(8,128)(2,1)} %all-gather.5.cloned.1.call-done, bf16[8192,128]{1,0:T(8,128)(2,1)} %all-gather.9.cloned.1.call-done), kind=kOutput, calls=%fused_computation.61 | convolution fusion | flops 1073741824 | bytes 10747904 | tf_op jit(solution)/shard_map/dot_general | solution.py:69
  283.8 3.1 fusion
  286.9 67.7 %all-gather.7.cloned.1.call-done = bf16[8192,128]{1,0:T(8,128)(2,1)} async-done(((bf16[256,128]{1,0:T(8,128)(2,1)}), bf16[8192,128]{1,0:T(8,128)(2,1)}) %all-gather.7.cloned.1.call-update) | async-done | bytes 2097168 | tf_op jit(solution)/shard_map/all_gather | solution.py:65
  354.5 8.8 %fusion.10 = bf16[512,1,4,128]{0,3,2,1:T(8,128)(2,1)S(1)} fusion(f32[4,512]{1,0:T(4,128)S(1)} %get-tuple-element.13, f32[512,512,4]{1,0,2:T(8,128)} %get-tuple-element.14, pred[512,512]{0,1:T(8,128)(4,1)S(1)} %fusion.15, bf16[512,8192]{1,0:T(8,128)(2,1)} %all-gather.5.cloned.1.call-done, bf16[8192,128]{1,0:T(8,128)(2,1)} %all-gather.7.cloned.1.call-done), kind=kOutput, calls=%fused_computation.14 | convolution fusion | flops 1346699264 | bytes 15474688 | tf_op jit(solution)/shard_map/grqk,kgd->qgrd/dot_general | solution.py:96
  363.9 18.0 %all_to_all.27 = bf16[8,64,512]{2,1,0:T(8,128)(2,1)S(1)} all-to-all(bf16[8,64,512]{2,1,0:T(8,128)(2,1)S(1)} %all_to_all.21), channel_id=1, replica_groups=mesh['dp'=32,'seq'=8] {'seq'}, dimensions={0} | all-to-all | bytes 1048576 | tf_op jit(solution)/shard_map/all_to_all | solution.py:100
  382.2 1.0 broadcast_in_dim.24
  (36 shorter events, 4.4 us)
Async XLA Ops:
  6.5 140.7 %all-gather.11.cloned.1.call-start = ((), (), s32[]{:S(2)}) async-start(), calls=%async_computation.6 | async-start | bytes 8650752 | tf_op jit(solution)/shard_map/all_gather | solution.py:63
  9.7 39.3 %all-to-all-start = ((bf16[32,1,1]{2,1,0:T(2,128)(2,1)}), bf16[32,1,1]{2,1,0:T(2,128)(2,1)S(1)}, u32[]{:S(2)}, u32[]{:S(2)}) async-start(bf16[32,1,1]{2,1,0:T(2,128)(2,1)} %copy.45), calls=%async_computation | async-start | bytes 32768 | tf_op jit(solution)/shard_map/all_to_all | solution.py:44
  49.0 79.4 %copy-start = (f32[8192]{0:T(1024)S(1)}, f32[8192]{0:T(1024)}, u32[]{:S(2)}) copy-start(f32[8192]{0:T(1024)} %param.10) | copy-start | bytes 98308
  49.0 72.7 %all-to-all-start.1 = ((bf16[32,3,8192]{2,1,0:T(4,128)(2,1)}), bf16[32,3,8192]{2,1,0:T(4,128)(2,1)S(1)}, u32[]{:S(2)}, u32[]{:S(2)}) async-start(bf16[32,3,8192]{2,1,0:T(4,128)(2,1)} %copy.47), calls=%async_computation.1 | async-start | bytes 4194304 | tf_op jit(solution)/shard_map/all_to_all | solution.py:43
  58.4 142.2 %all-gather.5.cloned.1.call-start = ((), (), s32[]{:S(2)}) async-start(), calls=%async_computation.3 | async-start | bytes 9437184 | tf_op jit(solution)/shard_map/all_gather | solution.py:61
  59.5 72.0 %copy-start.1 = (s32[1,512]{1,0:T(1,128)S(1)}, s32[1,512]{1,0:T(1,128)}, u32[]{:S(2)}) copy-start(s32[1,512]{1,0:T(1,128)} %param.9) | copy-start | bytes 6148
  129.6 147.3 %all-gather.9.cloned.1.call-start = ((), (), s32[]{:S(2)}) async-start(), calls=%async_computation.5 | async-start | bytes 2162688 | tf_op jit(solution)/shard_map/all_gather | solution.py:64
  130.4 224.2 %all-gather.7.cloned.1.call-start = ((), (), s32[]{:S(2)}) async-start(), calls=%async_computation.4 | async-start | bytes 2162688 | tf_op jit(solution)/shard_map/all_gather | solution.py:65
Sparse Core Ops, SparseCore 0:
  10.0 137.2 all-gather.10
  149.1 51.4 all-gather.4
  203.2 73.7 all-gather.8
  279.4 75.1 all-gather.6
where the time goes:
time: 390 us
  waiting for transfers between devices  267 us (68%)
  local copies, waits for them, and re-layouts  35.8 us (9%)
  matrix products  28.1 us (7%)
  starting transfers between devices  21.6 us (6%)
  blocking collectives  18 us (5%)
  between operations  13.3 us (3%)
  other arithmetic  6.2 us (2%)
    all_gather x1, waiting for transfers between devices, shards(): lax.all_gather(value_weight, 'dp', axis=0, tiled=True)  67.7 us
    all_gather x1, waiting for transfers between devices, shards(): lax.all_gather(key_weight, 'dp', axis=0, tiled=True)  66.4 us
    all_to_all x1, waiting for transfers between devices, shards(): lax.all_to_all(outgoing, 'dp', split_axis=0, concat_axis=0, tiled=True)  62.1 us
    all_gather x1, waiting for transfers between devices, shards(): lax.all_gather(normalize(placed, norm_gain), 'seq', axis=0, tiled=True)  53.4 us
    scatter x2, local copies, waits for them, and re-layouts, shards(): jnp.zeros((dp_count, capacity, row_width), jnp.bfloat16)  26.6 us
    all_to_all x1, blocking collectives, shards(): lax.all_to_all(pieces_out, 'seq', split_axis=0, concat_axis=1, tiled=True)  18 us
    dot_general x2, matrix products, shards(): jnp.dot(input_normed, one_piece, preferred_element_type=jnp.float32)  16.3 us
    all_gather x1, waiting for transfers between devices, shards(): lax.all_gather(w_query, 'dp', axis=0, tiled=True)  15.4 us
  transfers between devices with their start and end apart: 6, of which 5 were waited for; matrix products, arithmetic and copies ran while one was open for 15% of the time, Pallas kernels for 0%

commit v1 on v0

--- a/solution.py
+++ b/solution.py
@@ -6,6 +6,34 @@
 HEAD_SIZE = 128
 epsilon = 1e-05
 rope_base = 500000.0
+
+
+def direct_the_sizes(original):
+    axis_name = "seq"
+    r2 = lax.axis_size(axis_name)
+    g_now = lax.axis_index(axis_name)
+    row_out, r1, y1 = (r2, g_now, original.shape[0])
+    part_now = jnp.zeros(
+        [src_i * row_out if idx == 0 else src_i for idx, src_i in enumerate(original.shape)],
+        original.dtype,
+    )
+    y_new = lax.dynamic_update_slice_in_dim(part_now, original, r1 * y1, axis=0)
+    opened = raw_out = original
+    for no in [*range(1, row_out // 2 + 1)]:
+        opened = lax.ppermute(
+            opened, axis_name=axis_name, perm=[(idx, (idx + 1) % row_out) for idx in range(row_out)]
+        )
+        y_new = lax.dynamic_update_slice_in_dim(y_new, opened, (r1 - no) % row_out * y1, axis=0)
+        if 2 * no < row_out:
+            raw_out = lax.ppermute(
+                raw_out,
+                axis_name=axis_name,
+                perm=[(idx, (idx - 1) % row_out) for idx in range(row_out)],
+            )
+            y_new = lax.dynamic_update_slice_in_dim(
+                y_new, raw_out, (r1 + no) % row_out * y1, axis=0
+            )
+    return y_new
 
 
 def rotary_angles(values, token_positions):
@@ -58,7 +86,7 @@
     length = seg_all.shape[0]
     query_cols = w_query.shape[1]
     key_cols = key_weight.shape[1]
-    input_normed = lax.all_gather(normalize(placed, norm_gain), "seq", axis=0, tiled=True)
+    input_normed = direct_the_sizes(normalize(placed, norm_gain))
     pieces = (
         lax.all_gather(w_query, "dp", axis=0, tiled=True),
         lax.all_gather(key_weight, "dp", axis=0, tiled=True),

time: 390 us -> 315 us (0.81)
  waiting for transfers between devices: 267 us -> 165 us
  local copies, waits for them, and re-layouts: 35.8 us -> 49 us
  starting transfers between devices: 21.6 us -> 32.8 us
    all_gather x1, waiting for transfers between devices: 66.4 us -> 0.01 us  [shards(): lax.all_gather(key_weight, 'dp', axis=0, tiled=True)]
    all_gather x1 -> x0, waiting for transfers between devices: 53.4 us -> none  [shards(): lax.all_gather(normalize(placed, norm_gain), 'seq', axis=0, tiled=True)]
    ppermute x0 -> x7, waiting for transfers between devices: none -> 37 us  [the longest x4 35.6 us: direct_the_sizes(): lax.ppermute(opened, axis_name=axis_name, perm=[(idx, (idx + 1) % row_out...]
    ppermute x0 -> x7, starting transfers between devices: none -> 11.6 us  [the longest x4 11 us: direct_the_sizes(): lax.ppermute(opened, axis_name=axis_name, perm=[(idx, (idx + 1) % row_out...]
    dynamic_update_slice x0 -> x7, local copies, waits for them, and re-layouts: none -> 7.44 us  [the longest x4 4.25 us: direct_the_sizes(): lax.dynamic_update_slice_in_dim(y_new, opened, (r1 - no) % row_out * y1,...]
    all_gather x1, waiting for transfers between devices: 67.7 us -> 60.3 us  [shards(): lax.all_gather(value_weight, 'dp', axis=0, tiled=True)]
    all_gather x1, waiting for transfers between devices: 15.4 us -> 9.1 us  [shards(): lax.all_gather(w_query, 'dp', axis=0, tiled=True)]
    all_to_all x1, waiting for transfers between devices: 62.1 us -> 57.4 us  [shards(): lax.all_to_all(outgoing, 'dp', split_axis=0, concat_axis=0, tiled=True)]
  transfers between devices with their start and end apart: 6 -> 12, of which waited for: 5 -> 10; matrix products, arithmetic and copies ran while one was open for 15% -> 23% of each run, Pallas kernels for 0% -> 0%
where the time goes in v1:
time: 315 us; the launch traced here: 314 us
  waiting for transfers between devices  165 us (52%)
  local copies, waits for them, and re-layouts  49 us (16%)
  starting transfers between devices  32.8 us (10%)
  matrix products  28.3 us (9%)
  blocking collectives  18 us (6%)
  between operations  13.5 us (4%)
  other arithmetic  7.66 us (2%)
    all_gather x1, waiting for transfers between devices, shards(): lax.all_gather(value_weight, 'dp', axis=0, tiled=True)  60.3 us
    all_to_all x1, waiting for transfers between devices, shards(): lax.all_to_all(outgoing, 'dp', split_axis=0, concat_axis=0, tiled=True)  57.4 us
    ppermute x4, waiting for transfers between devices, direct_the_sizes(): lax.ppermute(opened, axis_name=axis_name, perm=[(idx, (idx + 1) % row_out...  35.6 us
    scatter x2, local copies, waits for them, and re-layouts, shards(): jnp.zeros((dp_count, capacity, row_width), jnp.bfloat16)  26.6 us
    all_to_all x1, blocking collectives, shards(): lax.all_to_all(pieces_out, 'seq', split_axis=0, concat_axis=1, tiled=True)  18 us
    dot_general x2, matrix products, shards(): jnp.dot(input_normed, one_piece, preferred_element_type=jnp.float32)  16.4 us
    all_to_all x1, starting transfers between devices, shards(): lax.all_to_all(counts.astype(jnp.bfloat16), 'dp', split_axis=0, concat_ax...  11.9 us
    ppermute x4, starting transfers between devices, direct_the_sizes(): lax.ppermute(opened, axis_name=axis_name, perm=[(idx, (idx + 1) % row_out...  11 us
  transfers between devices with their start and end apart: 12, of which 10 were waited for; matrix products, arithmetic and copies ran while one was open for 23% of the time, Pallas kernels for 0%

profile of v1, /device:TPU:1, one launch (start us, length us, event | category | flops | bytes accessed | tf_op | source)
XLA Modules:
  0.0 314.4 jit_solution(15166218403769954020)
XLA Ops:
  10.4 11.9 %all-to-all-start = ((bf16[32,1,1]{2,1,0:T(2,128)(2,1)}), bf16[32,1,1]{2,1,0:T(2,128)(2,1)S(1)}, u32[]{:S(2)}, u32[]{:S(2)}) async-start(bf16[32,1,1]{2,1,0:T(2,128)(2,1)} %copy.45), calls=%async_computation | async-start | bytes 32768 | tf_op jit(solution)/shard_map/all_to_all | solution.py:72
  23.1 23.9 %scatter_fusion = bf16[32,3,8192]{2,0,1:T(8,128)(2,1)S(1)} fusion(bf16[32,3,8192]{2,0,1:T(8,128)(2,1)S(1)} %broadcast_in_dim.24, s32[64]{0:T(128)S(1)} %fusion.28, bf16[64,8192]{1,0:T(8,128)(2,1)} %bitcast.80), kind=kCustom, calls=%fused_computation | custom fusion | bytes 3146240 | tf_op jit(solution)/shard_map/scatter | solution.py:68
  47.0 2.7 copy.47
  49.7 9.3 %all-to-all-start.1 = ((bf16[32,3,8192]{2,1,0:T(4,128)(2,1)}), bf16[32,3,8192]{2,1,0:T(4,128)(2,1)S(1)}, u32[]{:S(2)}, u32[]{:S(2)}) async-start(bf16[32,3,8192]{2,1,0:T(4,128)(2,1)} %copy.47), calls=%async_computation.1 | async-start | bytes 4194304 | tf_op jit(solution)/shard_map/all_to_all | solution.py:71
  60.1 57.4 %all-to-all-done.1 = bf16[32,3,8192]{2,1,0:T(4,128)(2,1)S(1)} async-done(((bf16[32,3,8192]{2,1,0:T(4,128)(2,1)}), bf16[32,3,8192]{2,1,0:T(4,128)(2,1)S(1)}, u32[]{:S(2)}, u32[]{:S(2)}) %all-to-all-start.1) | async-done | bytes 1572896 | tf_op jit(solution)/shard_map/all_to_all | solution.py:71
  117.5 2.6 reshape.239
  120.1 4.0 %scatter_custom_fusion.1 = bf16[64,8192]{1,0:T(8,128)(2,1)S(1)} fusion(s32[96]{0:T(128)S(1)} %fusion.27, bf16[96,8192]{1,0:T(8,128)(2,1)} %reshape.239, bf16[]{:T(256)} %constant.70.clone.1), kind=kCustom, calls=%fused_computation.24 | custom fusion | bytes 1049088 | tf_op jit(solution)/shard_map/scatter | solution.py:83
  124.4 4.2 %broadcast_in_dim.20 = bf16[512,8192]{1,0:T(8,128)(2,1)} broadcast(bf16[]{:T(256)} %constant.70.clone.1), dimensions={} | broadcast | bytes 8388610 | tf_op jit(solution)/shard_map/broadcast_in_dim | solution.py:16
  128.7 1.3 constant_dynamic-update-slice_fusion.7
  130.0 3.5 %collective-permute-start = (bf16[64,8192]{1,0:T(8,128)(2,1)S(1)}, bf16[64,8192]{1,0:T(8,128)(2,1)S(1)}, u32[]{:S(2)}, u32[]{:S(2)}) collective-permute-start(bf16[64,8192]{1,0:T(8,128)(2,1)S(1)} %get-tuple-element.8), channel_id=1, source_target_pairs={{0,1},{1,2},{2,3},{3,4},{4,5},{5,6},{6,7},{7,0},{8,9},{9,10},{10,1... | collective-permute-start | bytes 3145736 | tf_op jit(solution)/shard_map/ppermute | solution.py:23
  136.6 8.7 %collective-permute-done = bf16[64,8192]{1,0:T(8,128)(2,1)S(1)} collective-permute-done((bf16[64,8192]{1,0:T(8,128)(2,1)S(1)}, bf16[64,8192]{1,0:T(8,128)(2,1)S(1)}, u32[]{:S(2)}, u32[]{:S(2)}) %collective-permute-start) | collective-permute-done | bytes 1048608 | tf_op jit(solution)/shard_map/ppermute | solution.py:23
  145.3 2.5 collective-permute-start.2
  150.3 9.2 %collective-permute-done.2 = bf16[64,8192]{1,0:T(8,128)(2,1)S(1)} collective-permute-done((bf16[64,8192]{1,0:T(8,128)(2,1)S(1)}, bf16[64,8192]{1,0:T(8,128)(2,1)S(1)}, u32[]{:S(2)}, u32[]{:S(2)}) %collective-permute-start.2) | collective-permute-done | bytes 1048608 | tf_op jit(solution)/shard_map/ppermute | solution.py:23
  159.5 2.5 collective-permute-start.4
  165.4 8.3 %collective-permute-done.4 = bf16[64,8192]{1,0:T(8,128)(2,1)S(1)} collective-permute-done((bf16[64,8192]{1,0:T(8,128)(2,1)S(1)}, bf16[64,8192]{1,0:T(8,128)(2,1)S(1)}, u32[]{:S(2)}, u32[]{:S(2)}) %collective-permute-start.4) | collective-permute-done | bytes 1048608 | tf_op jit(solution)/shard_map/ppermute | solution.py:23
  173.7 2.5 collective-permute-start.6
  178.5 9.4 %collective-permute-done.6 = bf16[64,8192]{1,0:T(8,128)(2,1)S(1)} collective-permute-done((bf16[64,8192]{1,0:T(8,128)(2,1)S(1)}, bf16[64,8192]{1,0:T(8,128)(2,1)S(1)}, u32[]{:S(2)}, u32[]{:S(2)}) %collective-permute-start.6) | collective-permute-done | bytes 1048608 | tf_op jit(solution)/shard_map/ppermute | solution.py:23
  189.0 7.0 %fusion.33 = f32[512,128]{0,1:T(8,128)S(1)} fusion(bf16[512,8192]{1,0:T(8,128)(2,1)} %constant_dynamic-update-slice_fusion, bf16[8192,128]{1,0:T(8,128)(2,1)} %all-gather.6.cloned.1.call-done), kind=kOutput, calls=%fused_computation.69 | convolution fusion | flops 1073741824 | bytes 10747904 | tf_op jit(solution)/shard_map/dot_general | solution.py:97
  196.0 9.1 %all-gather.8.cloned.1.call-done = bf16[8192,512]{1,0:T(8,128)(2,1)} async-done(((bf16[256,512]{1,0:T(8,128)(2,1)}), bf16[8192,512]{1,0:T(8,128)(2,1)}) %all-gather.8.cloned.1.call-update) | async-done | bytes 8388624 | tf_op jit(solution)/shard_map/all_gather | solution.py:91
  205.1 9.4 %fusion.34 = f32[512,512]{0,1:T(8,128)S(1)} fusion(bf16[512,8192]{1,0:T(8,128)(2,1)} %constant_dynamic-update-slice_fusion, bf16[8192,512]{1,0:T(8,128)(2,1)} %all-gather.8.cloned.1.call-done), kind=kOutput, calls=%fused_computation.70 | convolution fusion | flops 4294967296 | bytes 17825792 | tf_op jit(solution)/shard_map/dot_general | solution.py:97
  215.8 3.1 fusion
  218.9 60.3 %all-gather.4.cloned.1.call-done = bf16[8192,128]{1,0:T(8,128)(2,1)} async-done(((bf16[256,128]{1,0:T(8,128)(2,1)}), bf16[8192,128]{1,0:T(8,128)(2,1)}) %all-gather.4.cloned.1.call-update) | async-done | bytes 2097168 | tf_op jit(solution)/shard_map/all_gather | solution.py:93
  279.2 8.8 %fusion.10 = bf16[512,1,4,128]{0,3,2,1:T(8,128)(2,1)S(1)} fusion(f32[4,512]{1,0:T(4,128)S(1)} %get-tuple-element.15, f32[512,512,4]{1,0,2:T(8,128)} %get-tuple-element.16, pred[512,512]{0,1:T(8,128)(4,1)S(1)} %copy-done.3, bf16[512,8192]{1,0:T(8,128)(2,1)} %constant_dynamic-update-slice_fusion, bf16[8192,128]{1,0:T(8,128)(2,1)} %all-gather.4.cloned.1.call-done), kind=kOutput, calls=%fused_computation.14 | convolution fusion | flops 1346699264 | bytes 15474688 | tf_op jit(solution)/shard_map/grqk,kgd->qgrd/dot_general | solution.py:124
  288.5 18.0 %all_to_all.27 = bf16[8,64,512]{2,1,0:T(8,128)(2,1)S(1)} all-to-all(bf16[8,64,512]{2,1,0:T(8,128)(2,1)S(1)} %all_to_all.21), channel_id=1, replica_groups=mesh['dp'=32,'seq'=8] {'seq'}, dimensions={0} | all-to-all | bytes 1048576 | tf_op jit(solution)/shard_map/all_to_all | solution.py:128
  (64 shorter events, 21.3 us)
Async XLA Ops:
  6.5 182.5 %all-gather.6.cloned.1.call-start = ((), (), s32[]{:S(2)}) async-start(), calls=%async_computation.4 | async-start | bytes 2162688 | tf_op jit(solution)/shard_map/all_gather | solution.py:92
  7.3 197.8 %all-gather.8.cloned.1.call-start = ((), (), s32[]{:S(2)}) async-start(), calls=%async_computation.5 | async-start | bytes 8650752 | tf_op jit(solution)/shard_map/all_gather | solution.py:91
  10.4 39.3 %all-to-all-start = ((bf16[32,1,1]{2,1,0:T(2,128)(2,1)}), bf16[32,1,1]{2,1,0:T(2,128)(2,1)S(1)}, u32[]{:S(2)}, u32[]{:S(2)}) async-start(bf16[32,1,1]{2,1,0:T(2,128)(2,1)} %copy.45), calls=%async_computation | async-start | bytes 32768 | tf_op jit(solution)/shard_map/all_to_all | solution.py:72
  49.7 67.8 %all-to-all-start.1 = ((bf16[32,3,8192]{2,1,0:T(4,128)(2,1)}), bf16[32,3,8192]{2,1,0:T(4,128)(2,1)S(1)}, u32[]{:S(2)}, u32[]{:S(2)}) async-start(bf16[32,3,8192]{2,1,0:T(4,128)(2,1)} %copy.47), calls=%async_computation.1 | async-start | bytes 4194304 | tf_op jit(solution)/shard_map/all_to_all | solution.py:71
  59.0 220.2 %all-gather.4.cloned.1.call-start = ((), (), s32[]{:S(2)}) async-start(), calls=%async_computation.3 | async-start | bytes 2162688 | tf_op jit(solution)/shard_map/all_gather | solution.py:93
  124.4 4.2 %copy-start.4 = (f32[8192]{0:T(1024)S(1)}, f32[8192]{0:T(1024)}, u32[]{:S(2)}) copy-start(f32[8192]{0:T(1024)} %param.10) | copy-start | bytes 98308
  128.7 7.0 %copy-start.5 = (s32[1,512]{1,0:T(1,128)S(1)}, s32[1,512]{1,0:T(1,128)}, u32[]{:S(2)}) copy-start(s32[1,512]{1,0:T(1,128)} %param.9) | copy-start | bytes 6148
  130.0 15.3 %collective-permute-start = (bf16[64,8192]{1,0:T(8,128)(2,1)S(1)}, bf16[64,8192]{1,0:T(8,128)(2,1)S(1)}, u32[]{:S(2)}, u32[]{:S(2)}) collective-permute-start(bf16[64,8192]{1,0:T(8,128)(2,1)S(1)} %get-tuple-element.8), channel_id=1, source_target_pairs={{0,1},{1,2},{2,3},{3,4},{4,5},{5,6},{6,7},{7,0},{8,9},{9,10},{10,1... | collective-permute-start | bytes 3145736 | tf_op jit(solution)/shard_map/ppermute | solution.py:23
  133.5 14.6 %collective-permute-start.1 = (bf16[64,8192]{1,0:T(8,128)(2,1)S(1)}, bf16[64,8192]{1,0:T(8,128)(2,1)S(1)}, u32[]{:S(2)}, u32[]{:S(2)}) collective-permute-start(bf16[64,8192]{1,0:T(8,128)(2,1)S(1)} %get-tuple-element.8), channel_id=1, source_target_pairs={{0,7},{1,0},{2,1},{3,2},{4,3},{5,4},{6,5},{7,6},{8,15},{9,8},{10,9... | collective-permute-start | bytes 3145736 | tf_op jit(solution)/shard_map/ppermute | solution.py:28
  134.2 0.6 copy-start.1
  145.3 14.2 %collective-permute-start.2 = (bf16[64,8192]{1,0:T(8,128)(2,1)S(1)}, bf16[64,8192]{1,0:T(8,128)(2,1)S(1)}, u32[]{:S(2)}, u32[]{:S(2)}) collective-permute-start(bf16[64,8192]{1,0:T(8,128)(2,1)S(1)} %collective-permute-done), channel_id=1, source_target_pairs={{0,1},{1,2},{2,3},{3,4},{4,5},{5,6},{6,7},{7,0},{8,9},{9,10},{10,1... | collective-permute-start | bytes 3145736 | tf_op jit(solution)/shard_map/ppermute | solution.py:23
  148.2 14.6 %collective-permute-start.3 = (bf16[64,8192]{1,0:T(8,128)(2,1)S(1)}, bf16[64,8192]{1,0:T(8,128)(2,1)S(1)}, u32[]{:S(2)}, u32[]{:S(2)}) collective-permute-start(bf16[64,8192]{1,0:T(8,128)(2,1)S(1)} %collective-permute-done.1), channel_id=1, source_target_pairs={{0,7},{1,0},{2,1},{3,2},{4,3},{5,4},{6,5},{7,6},{8,15},{9,8},{10,9... | collective-permute-start | bytes 3145736 | tf_op jit(solution)/shard_map/ppermute | solution.py:28
  159.5 14.2 %collective-permute-start.4 = (bf16[64,8192]{1,0:T(8,128)(2,1)S(1)}, bf16[64,8192]{1,0:T(8,128)(2,1)S(1)}, u32[]{:S(2)}, u32[]{:S(2)}) collective-permute-start(bf16[64,8192]{1,0:T(8,128)(2,1)S(1)} %collective-permute-done.2), channel_id=1, source_target_pairs={{0,1},{1,2},{2,3},{3,4},{4,5},{5,6},{6,7},{7,0},{8,9},{9,10},{10,1... | collective-permute-start | bytes 3145736 | tf_op jit(solution)/shard_map/ppermute | solution.py:23
  162.8 14.6 %collective-permute-start.5 = (bf16[64,8192]{1,0:T(8,128)(2,1)S(1)}, bf16[64,8192]{1,0:T(8,128)(2,1)S(1)}, u32[]{:S(2)}, u32[]{:S(2)}) collective-permute-start(bf16[64,8192]{1,0:T(8,128)(2,1)S(1)} %collective-permute-done.3), channel_id=1, source_target_pairs={{0,7},{1,0},{2,1},{3,2},{4,3},{5,4},{6,5},{7,6},{8,15},{9,8},{10,9... | collective-permute-start | bytes 3145736 | tf_op jit(solution)/shard_map/ppermute | solution.py:28
  173.7 14.2 %collective-permute-start.6 = (bf16[64,8192]{1,0:T(8,128)(2,1)S(1)}, bf16[64,8192]{1,0:T(8,128)(2,1)S(1)}, u32[]{:S(2)}, u32[]{:S(2)}) collective-permute-start(bf16[64,8192]{1,0:T(8,128)(2,1)S(1)} %collective-permute-done.4), channel_id=1, source_target_pairs={{0,1},{1,2},{2,3},{3,4},{4,5},{5,6},{6,7},{7,0},{8,9},{9,10},{10,1... | collective-permute-start | bytes 3145736 | tf_op jit(solution)/shard_map/ppermute | solution.py:23
  214.5 1.0 copy-start
  214.5 1.2 copy-start.2
  214.6 1.2 copy-start.3
Sparse Core Ops, SparseCore 0:
  9.9 93.8 all-gather.5
  106.4 98.6 all-gather.7
  207.7 71.4 all-gather.3
